TPU v7x, 32 devices: a whole 2x2x4 slice. The times are simulated.
32 devices in a mesh: grp: 2 (over y), row: 4 (over x, core), col: 4 (over z).
Axes of the slice: x: 2, y: 2, z: 4, core: 2. Of those that a mesh axis runs over, the one named last changes fastest.
Arguments:
- level_one: bfloat16 [128, 256, 192], P(('grp', 'row'), 'col'), parts along dimension 0, may hold values from -6 to 6
- level_two: bfloat16 [64, 128, 384], P(('grp', 'row'), 'col'), parts along dimension 0, may hold values from -6 to 6
- level_three: bfloat16 [32, 64, 768], P(('grp', 'row'), None, 'col'), parts along dimension 0, may hold values from -6 to 6
- level_four: bfloat16 [16, 32, 1536], P(('grp', 'row'), None, 'col'), parts along dimension 0, may hold values from -10.5 to 10.5
- bin_weight: bfloat16 [4, 1536, 256], P(None, 'col'), may hold values from -0.21875 to 0.21875
- neck_feature: bfloat16 [3, 3, 1536, 256], P(None, None, 'col'), may hold values from -0.0546875 to 0.0546875
- neck_pooled: bfloat16 [3, 3, 1024, 256], P(None, None, 'col'), may hold values from -0.0546875 to 0.0546875
- lateral_one: bfloat16 [192, 256], replicated, may hold values from -0.625 to 0.625
- lateral_two: bfloat16 [384, 256], replicated, may hold values from -0.4375 to 0.4375
- lateral_three: bfloat16 [768, 256], replicated, may hold values from -0.3125 to 0.3125
- smooth_weight: bfloat16 [3, 3, 3, 256, 256], replicated, may hold values from -0.1875 to 0.1875
- join_weight: bfloat16 [3, 3, 1024, 256], replicated, may hold values from -0.09375 to 0.09375
- biases: float32 [12, 256], replicated, may hold values from -2 to 2
Outputs:
- joined: bfloat16 [128, 256, 256], P(('grp', 'row'), 'col'), parts along dimension 0
There are 2 independent parts, one for each index of `grp`. A program takes and returns all parts, laid end to end along the dimension named above; an argument that names none is the same for every part. Nothing has to cross between parts.
All inputs are finite; a program needn't handle non-finite values.
Results may differ from a plain program's by a relative error of at most 0.015.
Values may be sent and summed in bfloat16 or wider, within the bound.
No kernel may reach another device: no remote copies, remote signals or barrier semaphores. Data moves between devices by JAX's collectives and lax.ppermute only.
A program may use at most 64 MiB of HBM per device.

v0:
```python
import jax
import jax.numpy as jnp
from jax import lax
from jax.sharding import PartitionSpec as P

highest = lax.Precision.HIGHEST
bin_sides = (1, 2, 3, 6)
rim = 2
f32 = jnp.float32
bf16 = jnp.bfloat16


def others(value, axis):
    count = lax.axis_size(axis)
    for shift in range(1, count):
        yield lax.ppermute(value, axis, [(i, (i + shift) % count) for i in range(count)])


def windows_sum(padded, axis, dim, pitch, width, join):
    count = lax.axis_size(axis)
    here = lax.axis_index(axis)

    def window_for(target):
        return lax.dynamic_slice_in_dim(padded, target * pitch, width, dim)

    pieces = [window_for(here)]
    for shift in range(1, count):
        target = lax.rem(here + shift, count)
        pieces.append(
            lax.ppermute(window_for(target), axis, [(i, (i + shift) % count) for i in range(count)])
        )
    return join(pieces)


def edge_swap(low_out, high_out, axis):
    count = lax.axis_size(axis)
    forward = [(i, i + 1) for i in range(count - 1)]
    backward = [(target, source) for source, target in forward]
    return (lax.ppermute(high_out, axis, forward), lax.ppermute(low_out, axis, backward))


def cell_table(size):
    branch, row, col = ([], [], [])
    for number, side in enumerate(bin_sides):
        for i in range(side):
            for j in range(side):
                branch.append(number)
                row.append(i)
                col.append(j)
    return (
        jnp.array(branch, jnp.int32),
        jnp.array(row, jnp.int32),
        jnp.array(col, jnp.int32),
        jnp.array([bin_sides[b] for b in branch], jnp.int32),
    )


def pool_inside(index, side, extent):
    position = jnp.arange(extent, dtype=jnp.int32)[None, :]
    first = (index * extent // side)[:, None]
    end = (((index + 1) * extent + side - 1) // side)[:, None]
    inside = ((position >= first) & (position < end)).astype(f32)
    return (inside, (end - first).astype(f32))


def spread_weights(position, index, side, extent):
    sides = side.astype(f32)[None, :]
    source = (position.astype(f32)[:, None] + 0.5) * sides / extent - 0.5
    source = jnp.minimum(jnp.maximum(source, 0.0), sides - 1.0)
    return jnp.maximum(0.0, 1.0 - jnp.abs(source - index.astype(f32)[None, :]))


def stretch(first_out, length_out, first_in, length_in, factor, extent):
    output = (first_out + jnp.arange(length_out, dtype=jnp.int32)).astype(f32)
    source = jnp.clip((output + 0.5) / factor - 0.5, 0.0, extent - 1.0)
    targets = (first_in + jnp.arange(length_in, dtype=jnp.int32)).astype(f32)
    inside = ((output >= 0.0) & (output < extent * factor)).astype(f32)
    return jnp.maximum(0.0, 1.0 - jnp.abs(source[:, None] - targets[None, :])) * inside[:, None]


def conv(feature, weight, padding):
    return lax.conv_general_dilated(
        feature[None],
        weight,
        (1, 1),
        padding,
        dimension_numbers=("NHWC", "HWIO", "NHWC"),
        preferred_element_type=f32,
    )[0]


def project(feature, weight):
    height, breadth, channels = feature.shape
    result = jnp.dot(
        feature.reshape(height * breadth, channels), weight, preferred_element_type=f32
    )
    return result.reshape(height, breadth, -1)


def local(
    level_one,
    level_two,
    level_three,
    level_four,
    bin_weight,
    neck_feature,
    neck_pooled,
    lateral_one,
    lateral_two,
    lateral_three,
    smooth_weight,
    join_weight,
    biases,
):
    row_here = lax.axis_index("row")
    col_here = lax.axis_index("col")
    row_count = lax.axis_size("row")
    col_count = lax.axis_size("col")
    rows4, grid_cols, part_four = level_four.shape
    grid_rows = rows4 * row_count
    cols4 = grid_cols // col_count
    channels = bin_weight.shape[2]
    four = lax.all_gather(level_four, "row", axis=0, tiled=True)
    branch, cell_row, cell_col, cell_side = cell_table(None)
    cells = branch.shape[0]
    in_rows, row_size = pool_inside(cell_row, cell_side, grid_rows)
    in_cols, col_size = pool_inside(cell_col, cell_side, grid_cols)
    inside = (in_rows[:, :, None] * in_cols[:, None, :]).reshape(cells, -1).astype(bf16)
    pooled = jnp.dot(inside, four.reshape(-1, part_four), preferred_element_type=f32)
    pooled = (pooled / (row_size * col_size)).astype(bf16)
    terms = []
    offset = 0
    for number, side in enumerate(bin_sides):
        terms.append(
            jnp.dot(
                pooled[offset : offset + side * side],
                bin_weight[number],
                preferred_element_type=f32,
            )
        )
        offset += side * side
    bin_term = jnp.concatenate(terms, axis=0).astype(bf16)
    bin_total = bin_term.astype(f32)
    for other in others(bin_term, "col"):
        bin_total = bin_total + other.astype(f32)
    lat_one = jax.nn.relu(project(level_one, lateral_one) + biases[5]).astype(bf16)
    lat_two = jax.nn.relu(project(level_two, lateral_two) + biases[6]).astype(bf16)
    cols3 = level_three.shape[1] // col_count
    three_wide = windows_sum(
        jnp.pad(level_three, ((0, 0), (rim, rim), (0, 0))),
        "col",
        1,
        cols3,
        cols3 + 2 * rim,
        lambda pieces: pieces,
    )
    share_three = level_three.shape[2]
    three_sum = jnp.zeros((), f32)
    for shift, piece in enumerate(three_wide):
        source = lax.rem(col_here - shift + col_count, col_count)
        weight = lax.dynamic_slice_in_dim(lateral_three, source * share_three, share_three, 0)
        three_sum = three_sum + project(piece, weight)
    lat_three = jax.nn.relu(three_sum + biases[7])
    rows3 = level_three.shape[0]
    first_col3 = col_here * cols3 - rim
    place = first_col3 + jnp.arange(cols3 + 2 * rim, dtype=jnp.int32)
    in_three = ((place >= 0) & (place < cols3 * col_count))[None, :, None]
    lat_three = jnp.where(in_three, lat_three, 0.0).astype(bf16)
    levels = [lat_one, lat_two, lat_three]

    def pack(parts):
        return jnp.concatenate([p.reshape(-1, channels) for p in parts], axis=0)

    def unpack(packed, shapes):
        result, start = ([], 0)
        for shape in shapes:
            size = shape[0] * shape[1]
            result.append(packed[start : start + size].reshape(shape + (channels,)))
            start += size
        return result

    shapes = [(rim, level.shape[1]) for level in levels]
    above, below = edge_swap(
        pack([level[:rim] for level in levels]), pack([level[-rim:] for level in levels]), "row"
    )
    levels = [
        jnp.concatenate([a, level, b], axis=0)
        for a, level, b in zip(unpack(above, shapes), levels, unpack(below, shapes))
    ]
    sided = levels[:2]
    shapes = [(level.shape[0], rim) for level in sided]
    before, after = edge_swap(
        pack([level[:, :rim] for level in sided]), pack([level[:, -rim:] for level in sided]), "col"
    )
    wide_one, wide_two = [
        jnp.concatenate([a, level, b], axis=1)
        for a, level, b in zip(unpack(before, shapes), sided, unpack(after, shapes))
    ]
    wide_three = levels[2]
    first_row = row_here * rows4
    span = rows4 + 2 * rim + 2
    place_rows = first_row - rim - 1 + jnp.arange(span, dtype=jnp.int32)
    in_grid = ((place_rows >= 0) & (place_rows < grid_rows)).astype(f32)
    four_span = lax.dynamic_slice_in_dim(
        jnp.pad(four, ((rim + 1, rim + 1), (0, 0), (0, 0))), first_row, span, 0
    )
    binned = jax.nn.relu(bin_total + biases[branch])
    spread_rows = spread_weights(place_rows, cell_row, cell_side, grid_rows) * in_grid[:, None]
    spread_cols = spread_weights(
        jnp.arange(grid_cols, dtype=jnp.int32), cell_col, cell_side, grid_cols
    )
    spread = (spread_rows[:, None, :] * spread_cols[None, :, :]).reshape(-1, cells)
    share_ppm = neck_pooled.shape[2]
    branches = len(bin_sides)
    lane_branch = jnp.arange(branches * channels, dtype=jnp.int32) // channels
    sorted_bins = jnp.where(
        branch[:, None] == lane_branch[None, :], jnp.tile(binned, (1, branches)), 0.0
    )
    sorted_bins = lax.dynamic_slice_in_dim(sorted_bins, col_here * share_ppm, share_ppm, 1)
    ppm = jnp.dot(spread, sorted_bins, precision=highest).astype(bf16)
    ppm = ppm.reshape(span, grid_cols, share_ppm)
    around = ((0, 0), (1, 1))
    neck_term = conv(four_span, neck_feature, around) + conv(ppm, neck_pooled, around)
    neck_pad = jnp.pad(neck_term.astype(bf16), ((0, 0), (rim, rim), (0, 0)))
    top_sum = windows_sum(
        neck_pad,
        "col",
        1,
        cols4,
        cols4 + 2 * rim,
        lambda pieces: sum((p.astype(f32) for p in pieces)),
    )
    top = jax.nn.relu(top_sum + biases[4]).astype(bf16)

    def upscale(source, level_rows, level_cols, factor, border_in, border_out):
        high, wide = (source.shape[0], source.shape[1])
        out_high = level_rows * factor + 2 * border_out
        out_wide = level_cols * factor + 2 * border_out
        down = stretch(
            row_here * level_rows * factor - border_out,
            out_high,
            row_here * level_rows - border_in,
            high,
            factor,
            level_rows * row_count,
        )
        across = stretch(
            col_here * level_cols * factor - border_out,
            out_wide,
            col_here * level_cols - border_in,
            wide,
            factor,
            level_cols * col_count,
        )
        matrix = (down[:, None, :, None] * across[None, :, None, :]).reshape(
            out_high * out_wide, high * wide
        )
        result = jnp.dot(
            matrix.astype(bf16), source.reshape(high * wide, -1), preferred_element_type=f32
        )
        return result.reshape(out_high, out_wide, -1)

    rows2, cols2 = (level_two.shape[0], level_two.shape[1])
    rows1, cols1 = (level_one.shape[0], level_one.shape[1])
    pyr_three = (wide_three.astype(f32) + upscale(top, rows4, cols4, 2, rim, rim)).astype(bf16)
    pyr_two = (wide_two.astype(f32) + upscale(pyr_three, rows3, cols3, 2, rim, rim)).astype(bf16)
    pyr_one = (wide_one.astype(f32) + upscale(pyr_two, rows2, cols2, 2, rim, rim)).astype(bf16)
    valid = ((0, 0), (0, 0))
    smooth_one = jax.nn.relu(conv(pyr_one, smooth_weight[0], valid) + biases[8])
    smooth_two = jax.nn.relu(conv(pyr_two, smooth_weight[1], valid) + biases[9]).astype(bf16)
    smooth_three = jax.nn.relu(conv(pyr_three, smooth_weight[2], valid) + biases[10]).astype(bf16)

    def in_image(length, here, count):
        place = here * length - 1 + jnp.arange(length + 2, dtype=jnp.int32)
        return (place >= 0) & (place < length * count)

    mask = (
        in_image(rows1, row_here, row_count)[:, None]
        & in_image(cols1, col_here, col_count)[None, :]
    )
    smooth_one = jnp.where(mask[:, :, None], smooth_one, 0.0).astype(bf16)
    stacked_top = jnp.concatenate(
        [
            smooth_one,
            upscale(smooth_two, rows2, cols2, 2, 1, 1).astype(bf16),
            upscale(smooth_three, rows3, cols3, 4, 1, 1).astype(bf16),
            upscale(top, rows4, cols4, 8, rim, 1).astype(bf16),
        ],
        axis=2,
    )
    return jax.nn.relu(conv(stacked_top, join_weight, valid) + biases[11]).astype(bf16)


def solution(mesh):
    placed = (
        P(("grp", "row"), "col", None),
        P(("grp", "row"), "col", None),
        P(("grp", "row"), None, "col"),
        P(("grp", "row"), None, "col"),
        P(None, "col", None),
        P(None, None, "col", None),
        P(None, None, "col", None),
        P(),
        P(),
        P(),
        P(),
        P(),
        P(),
    )
    return jax.shard_map(
        local, mesh=mesh, in_specs=placed, out_specs=P(("grp", "row"), "col", None), check_vma=False
    )
```

profile of v0, /device:TPU:2, one launch (start us, length us, event | category | flops | bytes accessed | tf_op | source)
XLA Modules:
  0.0 111.6 jit_solution(11040737455989784107)
XLA Ops:
  0.0 5.9 %all_gather.3 = bf16[8,32,384]{2,1,0:T(8,128)(2,1)S(1)} all-gather(bf16[2,32,384]{2,1,0:T(8,128)(2,1)} %param.20), channel_id=1, replica_groups=mesh['grp'=2,'row'=4,'col'=4] {'row'}, dimensions={0}, use_global_device_ids=true | all-gather | bytes 245760 | tf_op jit(solution)/shard_map/all_gather | solution.py:123
  8.2 1.1 fusion.105
  9.2 1.1 convolution_convert_fusion.5
  10.3 1.1 convolution_convert_fusion.4
  11.4 1.1 %convolution_convert_fusion.3 = bf16[36,256]{1,0:T(8,128)(2,1)S(1)} fusion(bf16[4,384,256]{2,1,0:T(8,128)(2,1)} %param.21, bf16[50,384]{1,0:T(8,128)(2,1)S(1)} %fusion.56), kind=kOutput, calls=%fused_computation.70 | convolution fusion | flops 7087104 | bytes 245760 | tf_op jit(solution)/shard_map/dot_general | solution.py:135
  13.2 2.6 %collective-permute-start.8 = (bf16[50,256]{1,0:T(8,128)(2,1)}, bf16[50,256]{1,0:T(8,128)(2,1)}, u32[]{:S(2)}, u32[]{:S(2)}) collective-permute-start(bf16[50,256]{1,0:T(8,128)(2,1)} %pad_maximum_fusion.4), channel_id=1, source_target_pairs={{0,2},{1,3},{2,0},{3,1},{4,6},{5,7},{6,4},{7,5},{8,10},{9,11},{10,... | collective-permute-start | bytes 76808 | tf_op jit(solution)/shard_map/ppermute | solution.py:16
  15.8 1.6 %collective-permute-start.7 = (bf16[50,256]{1,0:T(8,128)(2,1)}, bf16[50,256]{1,0:T(8,128)(2,1)}, u32[]{:S(2)}, u32[]{:S(2)}) collective-permute-start(bf16[50,256]{1,0:T(8,128)(2,1)} %pad_maximum_fusion.4), channel_id=1, source_target_pairs={{0,1},{1,2},{2,3},{3,0},{4,5},{5,6},{6,7},{7,4},{8,9},{9,10},{10,1... | collective-permute-start | bytes 76808 | tf_op jit(solution)/shard_map/ppermute | solution.py:16
  17.3 2.2 %collective-permute-start.9 = (bf16[50,256]{1,0:T(8,128)(2,1)}, bf16[50,256]{1,0:T(8,128)(2,1)}, u32[]{:S(2)}, u32[]{:S(2)}) collective-permute-start(bf16[50,256]{1,0:T(8,128)(2,1)} %pad_maximum_fusion.4), channel_id=1, source_target_pairs={{0,3},{1,0},{2,1},{3,2},{4,7},{5,4},{6,5},{7,6},{8,11},{9,8},{10,9... | collective-permute-start | bytes 76808 | tf_op jit(solution)/shard_map/ppermute | solution.py:16
  19.6 1.7 %pad_dynamic-slice_fusion.6 = (bf16[4,20,192]{2,1,0:T(8,128)(2,1)}, bf16[4,20,192]{2,1,0:T(8,128)(2,1)}, bf16[4,20,192]{2,1,0:T(8,128)(2,1)}) fusion(s32[]{:T(128)S(6)} %select_n.84, bf16[4,64,192]{2,1,0:T(8,128)(2,1)} %param.19, s32[]{:T(128)S(6)} %select_n.82, s32[]{:T(128)S(6)} %select_n.86), kind=kLoop, calls=%fused_computation.149 | loop fusion | bytes 190476 | tf_op jit(solution)/shard_map/dynamic_slice | solution.py:24
  31.2 1.3 %fusion.23 = bf16[16,64,256]{2,1,0:T(8,128)(2,1)S(1)} fusion(bf16[16,64,192]{2,1,0:T(8,128)(2,1)} %param.17, f32[256]{0:T(256)S(1)} %bitcast.234, bf16[192,256]{1,0:T(8,128)(2,1)S(1)} %copy-done.44), kind=kOutput, calls=%fused_computation.33 | convolution fusion | flops 101449728 | bytes 1016832 | tf_op jit(solution)/shard_map/dot_general | solution.py:94
  36.1 1.1 fusion.130
  37.2 2.0 %convolution_select_fusion.3 = f32[6,8,5,256]{3,1,2,0:T(8,128)} fusion(bf16[3,3,384,256]{3,2,1,0:T(8,128)(2,1)S(1)} %copy-done, bf16[8,1,7,2,384]{4,2,3,0,1:T(8,128)(2,1)S(1)} %slice.185, bf16[8,1,8,5,384]{4,2,3,0,1:T(8,128)(2,1)S(1)} %copy.121, pred[8,5]{0,1:T(8,128)(4,1)} %constant.322), kind=kOutput, calls=%fused_computation.51 | convolution fusion | flops 425766912 | bytes 2347048 | tf_op jit(solution)/shard_map/conv_general_dilated | solution.py:82
  45.3 3.2 %collective-permute-start.2 = (bf16[4,20,192]{2,1,0:T(8,128)(2,1)}, bf16[4,20,192]{2,1,0:T(8,128)(2,1)S(1)}, u32[]{:S(2)}, u32[]{:S(2)}) collective-permute-start(bf16[4,20,192]{2,1,0:T(8,128)(2,1)} %get-tuple-element.15), channel_id=1, source_target_pairs={{0,3},{1,0},{2,1},{3,2},{4,7},{5,4},{6,5},{7,6},{8,11},{9,8},{10,9... | collective-permute-start | bytes 92168 | tf_op jit(solution)/shard_map/ppermute | solution.py:30
  49.5 1.1 convolution_convert_fusion.2
  50.8 1.2 %fusion.37 = bf16[6,8,5,256]{3,1,2,0:T(8,128)(2,1)S(1)} fusion(f32[6,8,5,256]{3,1,2,0:T(8,128)S(1)} %copy-done.49, bf16[3,3,256,256]{3,2,1,0:T(8,128)(2,1)S(1)} %copy-done.43, bf16[8,1,7,2,256]{4,2,3,0,1:T(8,128)(2,1)S(1)} %slice.190, bf16[8,1,8,5,256]{4,2,3,0,1:T(8,128)(2,1)S(1)} %copy.124, pred[8,5]{0,1:T(8,128)(4,1)} %constant.322), kind=kOutput, calls=%fused_computation.55 | convolution fusion | flops 283987968 | bytes 1769512 | tf_op jit(solution)/shard_map/conv_general_dilated | solution.py:82
  52.7 1.1 %collective-permute-start.11 = (bf16[6,12,256]{2,0,1:T(8,128)(2,1)S(1)}, bf16[6,12,256]{2,0,1:T(8,128)(2,1)S(1)}, u32[]{:S(2)}, u32[]{:S(2)}) collective-permute-start(bf16[6,12,256]{2,0,1:T(8,128)(2,1)S(1)} %get-tuple-element.17), channel_id=1, source_target_pairs={{0,2},{1,3},{2,0},{3,1},{4,6},{5,7},{6,4},{7,5},{8,10},{9,11},{10,... | collective-permute-start | bytes 110600 | tf_op jit(solution)/shard_map/ppermute | solution.py:30
  53.9 2.9 %collective-permute-start.12 = (bf16[6,12,256]{2,0,1:T(8,128)(2,1)S(1)}, bf16[6,12,256]{2,0,1:T(8,128)(2,1)S(1)}, u32[]{:S(2)}, u32[]{:S(2)}) collective-permute-start(bf16[6,12,256]{2,0,1:T(8,128)(2,1)S(1)} %get-tuple-element.18), channel_id=1, source_target_pairs={{0,3},{1,0},{2,1},{3,2},{4,7},{5,4},{6,5},{7,6},{8,11},{9,8},{10,9... | collective-permute-start | bytes 110600 | tf_op jit(solution)/shard_map/ppermute | solution.py:30
  58.2 1.9 %collective-permute-start.4 = (bf16[232,256]{1,0:T(8,128)(2,1)S(1)}, bf16[232,256]{1,0:T(8,128)(2,1)S(1)}, u32[]{:S(2)}, u32[]{:S(2)}) collective-permute-start(bf16[232,256]{1,0:T(8,128)(2,1)S(1)} %pad_maximum_fusion.1), channel_id=1, source_target_pairs={{4,0},{8,4},{12,8},{5,1},{9,5},{13,9},{6,2},{10,6},{14,10},{7,3},{... | collective-permute-start | bytes 356360 | tf_op jit(solution)/shard_map/ppermute | solution.py:39
  60.8 2.4 %collective-permute-start.3 = (bf16[232,256]{1,0:T(8,128)(2,1)}, bf16[232,256]{1,0:T(8,128)(2,1)S(1)}, u32[]{:S(2)}, u32[]{:S(2)}) collective-permute-start(bf16[232,256]{1,0:T(8,128)(2,1)} %pad_maximum_fusion), channel_id=1, source_target_pairs={{0,4},{4,8},{8,12},{1,5},{5,9},{9,13},{2,6},{6,10},{10,14},{3,7},{... | collective-permute-start | bytes 356360 | tf_op jit(solution)/shard_map/ppermute | solution.py:39
  64.6 2.6 %collective-permute-done.3 = bf16[232,256]{1,0:T(8,128)(2,1)S(1)} collective-permute-done((bf16[232,256]{1,0:T(8,128)(2,1)}, bf16[232,256]{1,0:T(8,128)(2,1)S(1)}, u32[]{:S(2)}, u32[]{:S(2)}) %collective-permute-start.3) | collective-permute-done | bytes 118816 | tf_op jit(solution)/shard_map/ppermute | solution.py:39
  71.0 1.3 %collective-permute-start.6 = (bf16[64,256]{1,0:T(8,128)(2,1)}, bf16[64,256]{1,0:T(8,128)(2,1)}, u32[]{:S(2)}, u32[]{:S(2)}) collective-permute-start(bf16[64,256]{1,0:T(8,128)(2,1)} %pad_maximum_fusion.3), channel_id=1, source_target_pairs={{1,0},{2,1},{3,2},{5,4},{6,5},{7,6},{9,8},{10,9},{11,10},{13,12},{... | collective-permute-start | bytes 98312 | tf_op jit(solution)/shard_map/ppermute | solution.py:39
  72.9 5.2 %collective-permute-start.5 = (bf16[64,256]{1,0:T(8,128)(2,1)}, bf16[64,256]{1,0:T(8,128)(2,1)}, u32[]{:S(2)}, u32[]{:S(2)}) collective-permute-start(bf16[64,256]{1,0:T(8,128)(2,1)} %pad_maximum_fusion.2), channel_id=1, source_target_pairs={{0,1},{1,2},{2,3},{4,5},{5,6},{6,7},{8,9},{9,10},{10,11},{12,13},{... | collective-permute-start | bytes 98312 | tf_op jit(solution)/shard_map/ppermute | solution.py:39
  78.1 1.0 add_convert_fusion.1
  79.9 1.6 %fusion.47 = bf16[6,8,3,256]{3,1,2,0:T(8,128)(2,1)S(1)} fusion(bf16[3,3,3,256,256]{4,3,2,1,0:T(8,128)(2,1)} %param.27, bf16[8,1,7,2,256]{4,2,3,0,1:T(8,128)(2,1)S(1)} %slice.196, bf16[8,1,8,3,256]{4,2,3,0,1:T(8,128)(2,1)S(1)} %copy.141, f32[256]{0:T(256)S(1)} %bitcast.233, pred[8,3]{0,1:T(4,128)(4,1)S(1)} %copy-done.48), kind=kOutput, calls=%fused_computation.59 | convolution fusion | flops 170508288 | bytes 1410072 | tf_op jit(solution)/shard_map/conv_general_dilated | solution.py:82
  84.9 1.4 %add_convert_fusion = bf16[12,36,256]{2,1,0:T(8,128)(2,1)S(1)} fusion(bf16[12,2,256]{2,1,0:T(2,128)(2,1)S(1)} %reshape.1210, bf16[2,32,256]{2,1,0:T(8,128)(2,1)S(1)} %bitcast.220, bf16[8,32,256]{2,1,0:T(8,128)(2,1)S(1)} %fusion.36, bf16[2,32,256]{2,1,0:T(8,128)(2,1)S(1)} %bitcast.222, bf16[12,2,256]{2,1,0:T(2,128)(2,1)S(1)} %reshape.1209, ...), kind=kOutput, calls=%fused_computation.93 | convolution fusion | flops 36854784 | bytes 527552 | tf_op jit(solution)/shard_map/dot_general | solution.py:258
  86.4 2.2 %fusion.68 = bf16[20,1,68,256]{3,2,0,1:T(8,128)(2,1)S(1)} fusion(bf16[20,2,256]{2,1,0:T(2,128)(2,1)S(1)} %reshape.1208, bf16[2,64,256]{2,1,0:T(8,128)(2,1)S(1)} %bitcast.215, bf16[16,64,256]{2,1,0:T(8,128)(2,1)} %copy-done.3, bf16[2,64,256]{2,1,0:T(8,128)(2,1)S(1)} %bitcast.217, bf16[20,2,256]{2,1,0:T(2,128)(2,1)S(1)} %reshape.1205, ...), kind=kOutput, calls=%fused_computation.85 | convolution fusion | flops 306163200 | bytes 1624576 | tf_op jit(solution)/shard_map/dot_general | solution.py:258
  90.0 1.9 %fusion.26 = bf16[10,8,5,256]{3,1,2,0:T(8,128)(2,1)S(1)} fusion(bf16[3,3,3,256,256]{4,3,2,1,0:T(8,128)(2,1)} %param.27, bf16[12,1,7,2,256]{4,2,3,0,1:T(8,128)(2,1)S(1)} %slice.194, bf16[12,1,8,5,256]{4,2,3,0,1:T(8,128)(2,1)S(1)} %copy.135, f32[256]{0:T(256)S(1)} %bitcast.232, pred[8,5]{0,1:T(8,128)(4,1)S(1)} %copy-done.47), kind=kOutput, calls=%fused_computation.38 | convolution fusion | flops 473300992 | bytes 1717288 | tf_op jit(solution)/shard_map/conv_general_dilated | solution.py:82
  93.8 3.4 %convolution_select_fusion = f32[18,8,9,256]{3,1,2,0:T(8,128)S(1)} fusion(bf16[3,3,3,256,256]{4,3,2,1,0:T(8,128)(2,1)} %param.27, bf16[20,1,7,2,256]{4,2,3,0,1:T(8,128)(2,1)} %slice.192, bf16[20,1,8,9,256]{4,2,3,0,1:T(8,128)(2,1)} %copy-done.2, pred[8,9]{0,1:T(8,128)(4,1)S(1)} %copy-done.46), kind=kOutput, calls=%fused_computation.23 | convolution fusion | flops 1531858944 | bytes 3407944 | tf_op jit(solution)/shard_map/conv_general_dilated | solution.py:82
  100.2 1.4 %copy.160 = bf16[18,1,66,1024]{3,0,2,1:T(8,128)(2,1)S(1)} copy(bf16[18,1,66,1024]{3,2,0,1:T(8,128)(2,1)S(1)} %maximum_bitcast_fusion) | data formatting | bytes 4866048
  102.3 1.5 %copy.147 = bf16[18,1,8,9,1024]{4,2,3,0,1:T(8,128)(2,1)S(1)} copy(bf16[18,1,8,9,1024]{4,0,3,2,1:T(8,128)(2,1)S(1)} %bitcast.197) | data formatting | bytes 5308416 | tf_op jit(solution)/shard_map/conv_general_dilated | solution.py:82
  103.9 5.7 %fusion.16 = f32[16,8,9,256]{3,1,2,0:T(8,128)S(1)} fusion(bf16[3,3,1024,256]{3,2,1,0:T(8,128)(2,1)S(1)} %bitcast.236, bf16[18,1,7,2,1024]{4,2,3,0,1:T(8,128)(2,1)S(1)} %slice.198, bf16[18,1,8,9,1024]{4,2,3,0,1:T(8,128)(2,1)S(1)} %copy.147, pred[8,9]{0,1:T(8,128)(4,1)S(1)} %copy-done.45), kind=kOutput, calls=%fused_computation.27 | convolution fusion | flops 5445844992 | bytes 9068616 | tf_op jit(solution)/shard_map/conv_general_dilated | solution.py:82
  110.3 1.4 %fusion.59 = bf16[16,64,256]{2,1,0:T(8,128)(2,1)} fusion(f32[16,1,64,256]{3,0,2,1:T(8,128)S(1)} %slice.199, f32[256]{0:T(256)S(1)} %bitcast.230), kind=kLoop, calls=%fused_computation.76 | loop fusion | flops 786432 | bytes 1573888 | tf_op jit(solution)/shard_map/convert_element_type | solution.py:291
  (274 shorter events, 43.2 us)
Async XLA Ops:
  0.0 37.2 %copy-start = (bf16[3,3,384,256]{3,2,1,0:T(8,128)(2,1)S(1)}, bf16[3,3,384,256]{3,2,1,0:T(8,128)(2,1)}, u32[]{:S(2)}) copy-start(bf16[3,3,384,256]{3,2,1,0:T(8,128)(2,1)} %param.22) | copy-start | bytes 5308420
  0.0 29.8 %copy-start.21 = (s32[50]{0:T(128)S(1)}, s32[50]{0:T(128)}, u32[]{:S(2)}) copy-start(s32[50]{0:T(128)} %constant.284.clone) | copy-start | bytes 604
  0.0 29.8 %copy-start.1 = (f32[12,256]{1,0:T(8,128)S(1)}, f32[12,256]{1,0:T(8,128)}, u32[]{:S(2)}) copy-start(f32[12,256]{1,0:T(8,128)} %param.29) | copy-start | bytes 36868
  0.0 30.5 %copy-start.7 = (bf16[384,256]{1,0:T(8,128)(2,1)S(1)}, bf16[384,256]{1,0:T(8,128)(2,1)}, u32[]{:S(2)}) copy-start(bf16[384,256]{1,0:T(8,128)(2,1)} %param.25) | copy-start | bytes 589828
  0.0 30.5 %copy-start.6 = (bf16[8,32,384]{2,1,0:T(8,128)(2,1)S(1)}, bf16[8,32,384]{2,1,0:T(8,128)(2,1)}, u32[]{:S(2)}) copy-start(bf16[8,32,384]{2,1,0:T(8,128)(2,1)} %param.18) | copy-start | bytes 589828
  11.4 19.8 %copy-start.44 = (bf16[192,256]{1,0:T(8,128)(2,1)S(1)}, bf16[192,256]{1,0:T(8,128)(2,1)}, u32[]{:S(2)}) copy-start(bf16[192,256]{1,0:T(8,128)(2,1)} %param.24) | copy-start | bytes 294916
  12.6 12.6 %copy-start.16 = (bf16[1,256]{1,0:T(2,128)(2,1)}, bf16[1,256]{1,0:T(2,128)(2,1)S(1)}, u32[]{:S(2)}) copy-start(bf16[1,256]{1,0:T(2,128)(2,1)S(1)} %dot_general.64) | copy-start | bytes 1540
  13.2 32.1 %collective-permute-start.8 = (bf16[50,256]{1,0:T(8,128)(2,1)}, bf16[50,256]{1,0:T(8,128)(2,1)}, u32[]{:S(2)}, u32[]{:S(2)}) collective-permute-start(bf16[50,256]{1,0:T(8,128)(2,1)} %pad_maximum_fusion.4), channel_id=1, source_target_pairs={{0,2},{1,3},{2,0},{3,1},{4,6},{5,7},{6,4},{7,5},{8,10},{9,11},{10,... | collective-permute-start | bytes 76808 | tf_op jit(solution)/shard_map/ppermute | solution.py:16
  15.8 32.7 %collective-permute-start.7 = (bf16[50,256]{1,0:T(8,128)(2,1)}, bf16[50,256]{1,0:T(8,128)(2,1)}, u32[]{:S(2)}, u32[]{:S(2)}) collective-permute-start(bf16[50,256]{1,0:T(8,128)(2,1)} %pad_maximum_fusion.4), channel_id=1, source_target_pairs={{0,1},{1,2},{2,3},{3,0},{4,5},{5,6},{6,7},{7,4},{8,9},{9,10},{10,1... | collective-permute-start | bytes 76808 | tf_op jit(solution)/shard_map/ppermute | solution.py:16
  17.3 31.2 %collective-permute-start.9 = (bf16[50,256]{1,0:T(8,128)(2,1)}, bf16[50,256]{1,0:T(8,128)(2,1)}, u32[]{:S(2)}, u32[]{:S(2)}) collective-permute-start(bf16[50,256]{1,0:T(8,128)(2,1)} %pad_maximum_fusion.4), channel_id=1, source_target_pairs={{0,3},{1,0},{2,1},{3,2},{4,7},{5,4},{6,5},{7,6},{8,11},{9,8},{10,9... | collective-permute-start | bytes 76808 | tf_op jit(solution)/shard_map/ppermute | solution.py:16
  21.3 36.7 %collective-permute-start.1 = (bf16[4,20,192]{2,1,0:T(8,128)(2,1)}, bf16[4,20,192]{2,1,0:T(8,128)(2,1)S(1)}, u32[]{:S(2)}, u32[]{:S(2)}) collective-permute-start(bf16[4,20,192]{2,1,0:T(8,128)(2,1)} %get-tuple-element.13), channel_id=1, source_target_pairs={{0,2},{1,3},{2,0},{3,1},{4,6},{5,7},{6,4},{7,5},{8,10},{9,11},{10,... | collective-permute-start | bytes 92168 | tf_op jit(solution)/shard_map/ppermute | solution.py:30
  21.3 32.6 %collective-permute-start = (bf16[4,20,192]{2,1,0:T(8,128)(2,1)}, bf16[4,20,192]{2,1,0:T(8,128)(2,1)}, u32[]{:S(2)}, u32[]{:S(2)}) collective-permute-start(bf16[4,20,192]{2,1,0:T(8,128)(2,1)} %get-tuple-element.14), channel_id=1, source_target_pairs={{0,1},{1,2},{2,3},{3,0},{4,5},{5,6},{6,7},{7,4},{8,9},{9,10},{10,1... | collective-permute-start | bytes 92168 | tf_op jit(solution)/shard_map/ppermute | solution.py:30
  31.0 5.2 %copy-start.4 = (bf16[4,64,192]{2,1,0:T(8,128)(2,1)S(1)}, bf16[4,64,192]{2,1,0:T(8,128)(2,1)}, u32[]{:S(2)}) copy-start(bf16[4,64,192]{2,1,0:T(8,128)(2,1)} %param.19) | copy-start | bytes 294916
  32.5 37.8 %copy-start.3 = (bf16[16,64,256]{2,1,0:T(8,128)(2,1)}, bf16[16,64,256]{2,1,0:T(8,128)(2,1)S(1)}, u32[]{:S(2)}) copy-start(bf16[16,64,256]{2,1,0:T(8,128)(2,1)S(1)} %fusion.23) | copy-start | bytes 1572868
  44.4 6.3 %copy-start.49 = (f32[6,8,5,256]{3,1,2,0:T(8,128)S(1)}, f32[6,8,5,256]{3,1,2,0:T(8,128)}, u32[]{:S(2)}) copy-start(f32[6,8,5,256]{3,1,2,0:T(8,128)} %convolution_select_fusion.3) | copy-start | bytes 737284
  44.4 6.3 %copy-start.43 = (bf16[3,3,256,256]{3,2,1,0:T(8,128)(2,1)S(1)}, bf16[3,3,256,256]{3,2,1,0:T(8,128)(2,1)}, u32[]{:S(2)}) copy-start(bf16[3,3,256,256]{3,2,1,0:T(8,128)(2,1)} %param.23) | copy-start | bytes 3538948
  45.3 12.5 %collective-permute-start.2 = (bf16[4,20,192]{2,1,0:T(8,128)(2,1)}, bf16[4,20,192]{2,1,0:T(8,128)(2,1)S(1)}, u32[]{:S(2)}, u32[]{:S(2)}) collective-permute-start(bf16[4,20,192]{2,1,0:T(8,128)(2,1)} %get-tuple-element.15), channel_id=1, source_target_pairs={{0,3},{1,0},{2,1},{3,2},{4,7},{5,4},{6,5},{7,6},{8,11},{9,8},{10,9... | collective-permute-start | bytes 92168 | tf_op jit(solution)/shard_map/ppermute | solution.py:30
  50.8 6.0 %copy-start.5 = (bf16[768,256]{1,0:T(8,128)(2,1)S(1)}, bf16[768,256]{1,0:T(8,128)(2,1)}, u32[]{:S(2)}) copy-start(bf16[768,256]{1,0:T(8,128)(2,1)} %param.26) | copy-start | bytes 1179652
  50.8 7.1 %copy-start.19 = (f32[1,256]{1,0:T(1,128)S(1)}, f32[1,256]{1,0:T(1,128)}, u32[]{:S(2)}) copy-start(f32[1,256]{1,0:T(1,128)} %get-tuple-element.25) | copy-start | bytes 3076
  50.8 7.1 %copy-start.26 = (pred[20]{0:T(512)(128)(4,1)S(1)}, pred[20]{0:T(512)(128)(4,1)}, u32[]{:S(2)}) copy-start(pred[20]{0:T(512)(128)(4,1)} %compare_and_fusion) | copy-start | bytes 64
  52.0 11.2 %copy-start.18 = (f32[1,256]{1,0:T(1,128)S(1)}, f32[1,256]{1,0:T(1,128)}, u32[]{:S(2)}) copy-start(f32[1,256]{1,0:T(1,128)} %get-tuple-element.24) | copy-start | bytes 3076
  52.7 10.4 %collective-permute-start.10 = (bf16[6,12,256]{2,0,1:T(8,128)(2,1)}, bf16[6,12,256]{2,0,1:T(8,128)(2,1)S(1)}, u32[]{:S(2)}, u32[]{:S(2)}) collective-permute-start(bf16[6,12,256]{2,0,1:T(8,128)(2,1)} %get-tuple-element.16), channel_id=1, source_target_pairs={{0,1},{1,2},{2,3},{3,0},{4,5},{5,6},{6,7},{7,4},{8,9},{9,10},{10,1... | collective-permute-start | bytes 110600 | tf_op jit(solution)/shard_map/ppermute | solution.py:30
  52.7 10.5 %collective-permute-start.11 = (bf16[6,12,256]{2,0,1:T(8,128)(2,1)S(1)}, bf16[6,12,256]{2,0,1:T(8,128)(2,1)S(1)}, u32[]{:S(2)}, u32[]{:S(2)}) collective-permute-start(bf16[6,12,256]{2,0,1:T(8,128)(2,1)S(1)} %get-tuple-element.17), channel_id=1, source_target_pairs={{0,2},{1,3},{2,0},{3,1},{4,6},{5,7},{6,4},{7,5},{8,10},{9,11},{10,... | collective-permute-start | bytes 110600 | tf_op jit(solution)/shard_map/ppermute | solution.py:30
  53.9 9.3 %collective-permute-start.12 = (bf16[6,12,256]{2,0,1:T(8,128)(2,1)S(1)}, bf16[6,12,256]{2,0,1:T(8,128)(2,1)S(1)}, u32[]{:S(2)}, u32[]{:S(2)}) collective-permute-start(bf16[6,12,256]{2,0,1:T(8,128)(2,1)S(1)} %get-tuple-element.18), channel_id=1, source_target_pairs={{0,3},{1,0},{2,1},{3,2},{4,7},{5,4},{6,5},{7,6},{8,11},{9,8},{10,9... | collective-permute-start | bytes 110600 | tf_op jit(solution)/shard_map/ppermute | solution.py:30
  58.1 20.0 %copy-start.15 = (f32[20,12]{0,1:T(8,128)S(1)}, f32[20,12]{0,1:T(8,128)}, u32[]{:S(2)}) copy-start(f32[20,12]{0,1:T(8,128)} %maximum_multiply_fusion.6) | copy-start | bytes 2884
  58.2 5.7 %collective-permute-start.4 = (bf16[232,256]{1,0:T(8,128)(2,1)S(1)}, bf16[232,256]{1,0:T(8,128)(2,1)S(1)}, u32[]{:S(2)}, u32[]{:S(2)}) collective-permute-start(bf16[232,256]{1,0:T(8,128)(2,1)S(1)} %pad_maximum_fusion.1), channel_id=1, source_target_pairs={{4,0},{8,4},{12,8},{5,1},{9,5},{13,9},{6,2},{10,6},{14,10},{7,3},{... | collective-permute-start | bytes 356360 | tf_op jit(solution)/shard_map/ppermute | solution.py:39
  60.8 6.4 %collective-permute-start.3 = (bf16[232,256]{1,0:T(8,128)(2,1)}, bf16[232,256]{1,0:T(8,128)(2,1)S(1)}, u32[]{:S(2)}, u32[]{:S(2)}) collective-permute-start(bf16[232,256]{1,0:T(8,128)(2,1)} %pad_maximum_fusion), channel_id=1, source_target_pairs={{0,4},{4,8},{8,12},{1,5},{5,9},{9,13},{2,6},{6,10},{10,14},{3,7},{... | collective-permute-start | bytes 356360 | tf_op jit(solution)/shard_map/ppermute | solution.py:39
  63.3 16.6 %copy-start.25 = (f32[1,256]{1,0:T(1,128)S(1)}, f32[1,256]{1,0:T(1,128)}, u32[]{:S(2)}) copy-start(f32[1,256]{1,0:T(1,128)} %get-tuple-element.28) | copy-start | bytes 3076
  63.9 16.0 %copy-start.48 = (pred[8,3]{0,1:T(4,128)(4,1)S(1)}, pred[8,3]{0,1:T(4,128)(4,1)}, u32[]{:S(2)}) copy-start(pred[8,3]{0,1:T(4,128)(4,1)} %constant.381) | copy-start | bytes 76
  71.0 11.0 %collective-permute-start.6 = (bf16[64,256]{1,0:T(8,128)(2,1)}, bf16[64,256]{1,0:T(8,128)(2,1)}, u32[]{:S(2)}, u32[]{:S(2)}) collective-permute-start(bf16[64,256]{1,0:T(8,128)(2,1)} %pad_maximum_fusion.3), channel_id=1, source_target_pairs={{1,0},{2,1},{3,2},{5,4},{6,5},{7,6},{9,8},{10,9},{11,10},{13,12},{... | collective-permute-start | bytes 98312 | tf_op jit(solution)/shard_map/ppermute | solution.py:39
  72.9 10.5 %collective-permute-start.5 = (bf16[64,256]{1,0:T(8,128)(2,1)}, bf16[64,256]{1,0:T(8,128)(2,1)}, u32[]{:S(2)}, u32[]{:S(2)}) collective-permute-start(bf16[64,256]{1,0:T(8,128)(2,1)} %pad_maximum_fusion.2), channel_id=1, source_target_pairs={{0,1},{1,2},{2,3},{4,5},{5,6},{6,7},{8,9},{9,10},{10,11},{12,13},{... | collective-permute-start | bytes 98312 | tf_op jit(solution)/shard_map/ppermute | solution.py:39
  81.5 4.9 %copy-start.14 = (f32[68,36]{0,1:T(8,128)S(1)}, f32[68,36]{0,1:T(8,128)}, u32[]{:S(2)}) copy-start(f32[68,36]{0,1:T(8,128)} %maximum_multiply_fusion.1) | copy-start | bytes 29380
  (33 other events, 83.4 us)
where the time goes:
time: 113 us; the launch traced here: 112 us
  matrix products  32 us (28%)
  local copies, waits for them, and re-layouts  25.5 us (23%)
  starting transfers between devices  25 us (22%)
  other arithmetic  19.2 us (17%)
  blocking collectives  5.94 us (5%)
  waiting for transfers between devices  2.6 us (2%)
  between operations  1.36 us (1%)
    conv_general_dilated x6, matrix products, conv(): lax.conv_general_dilated(feature[None], weight, (1, 1), padding, dimensio...  15.8 us
    ppermute x6, starting transfers between devices, windows_sum(): lax.ppermute(window_for(target), axis, [(i, (i + shift) % count) for i in...  7.87 us
    ppermute x2, starting transfers between devices, edge_swap(): lax.ppermute(high_out, axis, forward)  7.55 us
    ppermute x3, starting transfers between devices, others(): lax.ppermute(value, axis, [(i, (i + shift) % count) for i in range(count)])  6.41 us
    dot_general x6, matrix products, upscale(): jnp.dot(matrix.astype(bf16), source.reshape(high * wide, -1), preferred_e...  6.07 us
    all_gather x1, blocking collectives, local(): four = lax.all_gather(level_four, 'row', axis=0, tiled=True)  5.94 us
    slice x10, local copies, waits for them, and re-layouts, unpack(): result.append(packed[start:start + size].reshape(shape + (channels,)))  5.34 us
    dot_general x4, matrix products, local(): jnp.dot(pooled[offset:offset + side * side], bin_weight[number], preferre...  4.35 us
  transfers between devices with their start and end apart: 13, of which 1 were waited for; matrix products, arithmetic and copies ran while one was open for 33% of the time, Pallas kernels for 0%

commit v1 on v0

--- a/solution.py
+++ b/solution.py
@@ -120,7 +120,12 @@
     grid_rows = rows4 * row_count
     cols4 = grid_cols // col_count
     channels = bin_weight.shape[2]
-    four = lax.all_gather(level_four, "row", axis=0, tiled=True)
+    ring = [level_four]
+    for hop in range(3):
+        ring.append(lax.ppermute(ring[-1], "row", [(dev, (dev + 1) % 4) for dev in range(4)]))
+    four = jnp.roll(
+        jnp.concatenate(ring[::-1], axis=0), (lax.axis_index("row") + 1) * ring[0].shape[0], axis=0
+    )
     branch, cell_row, cell_col, cell_side = cell_table(None)
     cells = branch.shape[0]
     in_rows, row_size = pool_inside(cell_row, cell_side, grid_rows)

time: 113 us -> 99.6 us (0.88)
  the two profiles are of different devices: /device:TPU:2 before, /device:TPU:0 now
where the time goes in v1:
time: 99.6 us; the launch traced here: 98.5 us
  starting transfers between devices  28.5 us (29%)
  matrix products  27.7 us (28%)
  local copies, waits for them, and re-layouts  20.9 us (21%)
  other arithmetic  18.5 us (19%)
  waiting for transfers between devices  1.5 us (2%)
  between operations  1.5 us (2%)
    conv_general_dilated x6, matrix products, conv(): lax.conv_general_dilated(feature[None], weight, (1, 1), padding, dimensio...  15.1 us
    ppermute x6, starting transfers between devices, windows_sum(): lax.ppermute(window_for(target), axis, [(i, (i + shift) % count) for i in...  11.6 us
    ppermute x2, starting transfers between devices, edge_swap(): lax.ppermute(high_out, axis, forward)  8.79 us
    mul x11, other arithmetic, stretch(): jnp.maximum(0.0, 1.0 - jnp.abs(source[:, None] - targets[None, :]))  7.45 us
    dot_general x6, matrix products, project(): jnp.dot(feature.reshape(height * breadth, channels), weight, preferred_el...  5.61 us
    dot_general x6, matrix products, upscale(): jnp.dot(matrix.astype(bf16), source.reshape(high * wide, -1), preferred_e...  4.04 us
    ppermute x3, starting transfers between devices, others(): lax.ppermute(value, axis, [(i, (i + shift) % count) for i in range(count)])  3.95 us
    conv_general_dilated x16, local copies, waits for them, and re-layouts, conv(): lax.conv_general_dilated(feature[None], weight, (1, 1), padding, dimensio...  3.71 us
  transfers between devices with their start and end apart: 16, of which 1 were waited for; matrix products, arithmetic and copies ran while one was open for 40% of the time, Pallas kernels for 0%

profile of v1, /device:TPU:0, one launch (start us, length us, event | category | flops | bytes accessed | tf_op | source)
XLA Modules:
  0.0 98.5 jit_solution(754058119327782372)
XLA Ops:
  0.7 1.7 %pad_dynamic-slice_fusion.6 = (bf16[4,20,192]{2,1,0:T(8,128)(2,1)}, bf16[4,20,192]{2,1,0:T(8,128)(2,1)}, bf16[4,20,192]{2,1,0:T(8,128)(2,1)}) fusion(s32[]{:T(128)S(6)} %select_n.97, bf16[4,64,192]{2,1,0:T(8,128)(2,1)} %param.19, s32[]{:T(128)S(6)} %select_n.95, s32[]{:T(128)S(6)} %select_n.99), kind=kLoop, calls=%fused_computation.149 | loop fusion | bytes 190476 | tf_op jit(solution)/shard_map/dynamic_slice | solution.py:24
  2.3 3.7 %collective-permute-start.1 = (bf16[4,20,192]{2,1,0:T(8,128)(2,1)}, bf16[4,20,192]{2,1,0:T(8,128)(2,1)}, u32[]{:S(2)}, u32[]{:S(2)}) collective-permute-start(bf16[4,20,192]{2,1,0:T(8,128)(2,1)} %get-tuple-element.13), channel_id=1, source_target_pairs={{0,2},{1,3},{2,0},{3,1},{4,6},{5,7},{6,4},{7,5},{8,10},{9,11},{10,... | collective-permute-start | bytes 92168 | tf_op jit(solution)/shard_map/ppermute | solution.py:30
  6.1 1.6 %collective-permute-start = (bf16[4,20,192]{2,1,0:T(8,128)(2,1)}, bf16[4,20,192]{2,1,0:T(8,128)(2,1)}, u32[]{:S(2)}, u32[]{:S(2)}) collective-permute-start(bf16[4,20,192]{2,1,0:T(8,128)(2,1)} %get-tuple-element.14), channel_id=1, source_target_pairs={{0,1},{1,2},{2,3},{3,0},{4,5},{5,6},{6,7},{7,4},{8,9},{9,10},{10,1... | collective-permute-start | bytes 92168 | tf_op jit(solution)/shard_map/ppermute | solution.py:30
  7.7 2.2 %collective-permute-start.2 = (bf16[4,20,192]{2,1,0:T(8,128)(2,1)}, bf16[4,20,192]{2,1,0:T(8,128)(2,1)}, u32[]{:S(2)}, u32[]{:S(2)}) collective-permute-start(bf16[4,20,192]{2,1,0:T(8,128)(2,1)} %get-tuple-element.15), channel_id=1, source_target_pairs={{0,3},{1,0},{2,1},{3,2},{4,7},{5,4},{6,5},{7,6},{8,11},{9,8},{10,9... | collective-permute-start | bytes 92168 | tf_op jit(solution)/shard_map/ppermute | solution.py:30
  12.5 1.2 %pad_clamp_fusion = s32[1024]{0:T(1024)} fusion(s32[50]{0:T(128)} %constant.304.clone), kind=kLoop, calls=%fused_computation.223 | loop fusion | flops 1024 | bytes 4296 | tf_op jit(solution)/shard_map/gather | solution.py:212
  13.7 1.5 %fusion.194 = (f32[1,256]{1,0:T(1,128)}, f32[1,256]{1,0:T(1,128)}, f32[1,256]{1,0:T(1,128)}, f32[1,256]{1,0:T(1,128)}, f32[1,256]{1,0:T(1,128)}, /*index=5*/f32[...) fusion(f32[12,256]{1,0:T(8,128)} %param.29), kind=kLoop, calls=%fused_computation.312 | loop fusion | bytes 16384 | tf_op jit(solution)/shard_map/slice | solution.py:296
  15.2 1.2 %fusion.36 = bf16[8,32,256]{2,1,0:T(8,128)(2,1)S(1)} fusion(bf16[8,32,384]{2,1,0:T(8,128)(2,1)} %param.18, bf16[384,256]{1,0:T(8,128)(2,1)} %param.25, f32[256]{0:T(256)S(1)} %bitcast.229), kind=kOutput, calls=%fused_computation.52 | convolution fusion | flops 50528256 | bytes 525312 | tf_op jit(solution)/shard_map/dot_general | solution.py:94
  16.5 1.3 %fusion.23 = bf16[16,64,256]{2,1,0:T(8,128)(2,1)S(1)} fusion(bf16[16,64,192]{2,1,0:T(8,128)(2,1)} %param.17, f32[256]{0:T(256)S(1)} %bitcast.234, bf16[192,256]{1,0:T(8,128)(2,1)} %param.24), kind=kOutput, calls=%fused_computation.33 | convolution fusion | flops 101449728 | bytes 1016832 | tf_op jit(solution)/shard_map/dot_general | solution.py:94
  24.0 1.3 %maximum_multiply_fusion.9 = (f32[18,6]{0,1:T(8,128)}, f32[18,6]{0,1:T(8,128)}) fusion(f32[18]{0:T(128)S(1)} %get-tuple-element.33, f32[6]{0:T(128)} %add_convert_fusion.3, f32[18]{0:T(128)S(1)} %get-tuple-element.36, f32[6]{0:T(128)S(1)} %add_convert_fusion.7, f32[18]{0:T(128)S(1)} %get-tuple-element.35), kind=kLoop, calls=%fused_computation.229 | loop fusion | flops 1080 | bytes 1128 | tf_op jit(solution)/shard_map/mul | solution.py:78
  28.3 1.3 %dynamic-slice = s32[256]{0:T(256)} dynamic-slice(s32[1024]{0:T(1024)} %add_select_fusion, s32[]{:T(128)S(6)} %select_n.112), dynamic_slice_sizes={256} | dynamic-slice | bytes 2052 | tf_op jit(solution)/shard_map/dynamic_slice | solution.py:224
  29.6 1.0 convolution_add_fusion.3
  31.5 1.0 fusion.55
  33.2 1.4 %collective-permute-start.4 = (bf16[232,256]{1,0:T(8,128)(2,1)S(1)}, bf16[232,256]{1,0:T(8,128)(2,1)S(1)}, u32[]{:S(2)}, u32[]{:S(2)}) collective-permute-start(bf16[232,256]{1,0:T(8,128)(2,1)S(1)} %pad_maximum_fusion.1), channel_id=1, source_target_pairs={{4,0},{8,4},{12,8},{5,1},{9,5},{13,9},{6,2},{10,6},{14,10},{7,3},{... | collective-permute-start | bytes 356360 | tf_op jit(solution)/shard_map/ppermute | solution.py:39
  34.7 1.4 %collective-permute-done.8 = bf16[2,32,384]{2,1,0:T(8,128)(2,1)S(1)} collective-permute-done((bf16[2,32,384]{2,1,0:T(8,128)(2,1)S(1)}, bf16[2,32,384]{2,1,0:T(8,128)(2,1)S(1)}, u32[]{:S(2)}, u32[]{:S(2)}) %collective-permute-start.8) | collective-permute-done | bytes 49184 | tf_op jit(solution)/shard_map/ppermute | solution.py:125
  36.4 3.6 %collective-permute-start.3 = (bf16[232,256]{1,0:T(8,128)(2,1)S(1)}, bf16[232,256]{1,0:T(8,128)(2,1)S(1)}, u32[]{:S(2)}, u32[]{:S(2)}) collective-permute-start(bf16[232,256]{1,0:T(8,128)(2,1)S(1)} %pad_maximum_fusion), channel_id=1, source_target_pairs={{0,4},{4,8},{8,12},{1,5},{5,9},{9,13},{2,6},{6,10},{10,14},{3,7},{... | collective-permute-start | bytes 356360 | tf_op jit(solution)/shard_map/ppermute | solution.py:39
  41.2 1.1 %fusion.105 = f32[1,256]{1,0:T(1,128)S(1)} fusion(bf16[4,384,256]{2,1,0:T(8,128)(2,1)} %param.21, bf16[50,384]{1,0:T(8,128)(2,1)S(1)} %fusion.56), kind=kOutput, calls=%fused_computation.125 | convolution fusion | flops 196608 | bytes 199168 | tf_op jit(solution)/shard_map/dot_general | solution.py:140
  43.4 3.3 %collective-permute-start.12 = (bf16[50,256]{1,0:T(8,128)(2,1)S(1)}, bf16[50,256]{1,0:T(8,128)(2,1)S(1)}, u32[]{:S(2)}, u32[]{:S(2)}) collective-permute-start(bf16[50,256]{1,0:T(8,128)(2,1)S(1)} %pad_maximum_fusion.4), channel_id=1, source_target_pairs={{0,3},{1,0},{2,1},{3,2},{4,7},{5,4},{6,5},{7,6},{8,11},{9,8},{10,9... | collective-permute-start | bytes 76808 | tf_op jit(solution)/shard_map/ppermute | solution.py:16
  47.0 1.3 %convolution_select_fusion.3 = f32[6,8,5,256]{3,1,2,0:T(8,128)} fusion(bf16[3,3,384,256]{3,2,1,0:T(8,128)(2,1)S(1)} %copy-done, bf16[8,1,7,2,384]{4,2,3,0,1:T(8,128)(2,1)S(1)} %slice.185, bf16[8,1,8,5,384]{4,2,3,0,1:T(8,128)(2,1)S(1)} %copy.91, pred[8,5]{0,1:T(8,128)(4,1)S(1)} %copy-done.42), kind=kOutput, calls=%fused_computation.51 | convolution fusion | flops 425766912 | bytes 2347048 | tf_op jit(solution)/shard_map/conv_general_dilated | solution.py:82
  49.7 1.3 %collective-permute-start.6 = (bf16[64,256]{1,0:T(8,128)(2,1)}, bf16[64,256]{1,0:T(8,128)(2,1)}, u32[]{:S(2)}, u32[]{:S(2)}) collective-permute-start(bf16[64,256]{1,0:T(8,128)(2,1)} %pad_maximum_fusion.3), channel_id=1, source_target_pairs={{1,0},{2,1},{3,2},{5,4},{6,5},{7,6},{9,8},{10,9},{11,10},{13,12},{... | collective-permute-start | bytes 98312 | tf_op jit(solution)/shard_map/ppermute | solution.py:39
  51.6 5.1 %collective-permute-start.5 = (bf16[64,256]{1,0:T(8,128)(2,1)}, bf16[64,256]{1,0:T(8,128)(2,1)}, u32[]{:S(2)}, u32[]{:S(2)}) collective-permute-start(bf16[64,256]{1,0:T(8,128)(2,1)} %pad_maximum_fusion.2), channel_id=1, source_target_pairs={{0,1},{1,2},{2,3},{4,5},{5,6},{6,7},{8,9},{9,10},{10,11},{12,13},{... | collective-permute-start | bytes 98312 | tf_op jit(solution)/shard_map/ppermute | solution.py:39
  57.7 1.4 %fusion.37 = bf16[6,8,5,256]{3,1,2,0:T(8,128)(2,1)S(1)} fusion(f32[6,8,5,256]{3,1,2,0:T(8,128)} %convolution_select_fusion.3, bf16[3,3,256,256]{3,2,1,0:T(8,128)(2,1)S(1)} %copy-done.38, bf16[8,1,7,2,256]{4,2,3,0,1:T(8,128)(2,1)S(1)} %slice.190, bf16[8,1,8,5,256]{4,2,3,0,1:T(8,128)(2,1)S(1)} %copy.94, pred[8,5]{0,1:T(8,128)(4,1)S(1)} %copy-done.42), kind=kOutput, calls=%fused_computation.55 | convolution fusion | flops 283987968 | bytes 1769512 | tf_op jit(solution)/shard_map/conv_general_dilated | solution.py:82
  59.9 1.1 %collective-permute-start.14 = (bf16[6,12,256]{2,0,1:T(8,128)(2,1)}, bf16[6,12,256]{2,0,1:T(8,128)(2,1)S(1)}, u32[]{:S(2)}, u32[]{:S(2)}) collective-permute-start(bf16[6,12,256]{2,0,1:T(8,128)(2,1)} %get-tuple-element.17), channel_id=1, source_target_pairs={{0,2},{1,3},{2,0},{3,1},{4,6},{5,7},{6,4},{7,5},{8,10},{9,11},{10,... | collective-permute-start | bytes 110600 | tf_op jit(solution)/shard_map/ppermute | solution.py:30
  61.0 2.9 %collective-permute-start.15 = (bf16[6,12,256]{2,0,1:T(8,128)(2,1)}, bf16[6,12,256]{2,0,1:T(8,128)(2,1)}, u32[]{:S(2)}, u32[]{:S(2)}) collective-permute-start(bf16[6,12,256]{2,0,1:T(8,128)(2,1)} %get-tuple-element.18), channel_id=1, source_target_pairs={{0,3},{1,0},{2,1},{3,2},{4,7},{5,4},{6,5},{7,6},{8,11},{9,8},{10,9... | collective-permute-start | bytes 110600 | tf_op jit(solution)/shard_map/ppermute | solution.py:30
  71.9 1.0 add_convert_fusion.1
  73.0 1.6 %fusion.47 = bf16[6,8,3,256]{3,1,2,0:T(8,128)(2,1)S(1)} fusion(bf16[3,3,3,256,256]{4,3,2,1,0:T(8,128)(2,1)} %param.27, bf16[8,1,7,2,256]{4,2,3,0,1:T(8,128)(2,1)S(1)} %slice.196, bf16[8,1,8,3,256]{4,2,3,0,1:T(8,128)(2,1)S(1)} %copy.111, f32[256]{0:T(256)} %bitcast.233, pred[8,3]{0,1:T(4,128)(4,1)} %constant.401), kind=kOutput, calls=%fused_computation.59 | convolution fusion | flops 170508288 | bytes 1410560 | tf_op jit(solution)/shard_map/conv_general_dilated | solution.py:82
  75.3 1.1 %fusion.68 = bf16[20,1,68,256]{3,2,0,1:T(8,128)(2,1)S(1)} fusion(bf16[20,2,256]{2,1,0:T(2,128)(2,1)S(1)} %reshape.1208, bf16[2,64,256]{2,1,0:T(8,128)(2,1)S(1)} %bitcast.215, bf16[16,64,256]{2,1,0:T(8,128)(2,1)S(1)} %fusion.23, bf16[2,64,256]{2,1,0:T(8,128)(2,1)S(1)} %bitcast.217, bf16[20,2,256]{2,1,0:T(2,128)(2,1)S(1)} %reshape.1205, ...), kind=kOutput, calls=%fused_computation.85 | convolution fusion | flops 306163200 | bytes 1624576 | tf_op jit(solution)/shard_map/dot_general | solution.py:263
  77.9 1.9 %fusion.26 = bf16[10,8,5,256]{3,1,2,0:T(8,128)(2,1)S(1)} fusion(bf16[3,3,3,256,256]{4,3,2,1,0:T(8,128)(2,1)} %param.27, bf16[12,1,7,2,256]{4,2,3,0,1:T(8,128)(2,1)S(1)} %slice.194, bf16[12,1,8,5,256]{4,2,3,0,1:T(8,128)(2,1)S(1)} %copy.105, f32[256]{0:T(256)S(1)} %bitcast.232, pred[8,5]{0,1:T(8,128)(4,1)S(1)} %copy-done.41), kind=kOutput, calls=%fused_computation.38 | convolution fusion | flops 473300992 | bytes 1717288 | tf_op jit(solution)/shard_map/conv_general_dilated | solution.py:82
  80.0 3.1 %convolution_select_fusion = f32[18,8,9,256]{3,1,2,0:T(8,128)S(1)} fusion(bf16[3,3,3,256,256]{4,3,2,1,0:T(8,128)(2,1)} %param.27, bf16[20,1,7,2,256]{4,2,3,0,1:T(8,128)(2,1)} %slice.192, bf16[20,1,8,9,256]{4,2,3,0,1:T(8,128)(2,1)S(1)} %copy.99, pred[8,9]{0,1:T(8,128)(4,1)S(1)} %copy-done.40), kind=kOutput, calls=%fused_computation.23 | convolution fusion | flops 1531858944 | bytes 3407944 | tf_op jit(solution)/shard_map/conv_general_dilated | solution.py:82
  87.0 1.4 %copy.130 = bf16[18,1,66,1024]{3,0,2,1:T(8,128)(2,1)S(1)} copy(bf16[18,1,66,1024]{3,2,0,1:T(8,128)(2,1)S(1)} %maximum_bitcast_fusion) | data formatting | bytes 4866048
  89.0 1.5 %copy.117 = bf16[18,1,8,9,1024]{4,2,3,0,1:T(8,128)(2,1)S(1)} copy(bf16[18,1,8,9,1024]{4,0,3,2,1:T(8,128)(2,1)S(1)} %bitcast.197) | data formatting | bytes 5308416 | tf_op jit(solution)/shard_map/conv_general_dilated | solution.py:82
  90.7 5.7 %fusion.16 = f32[16,8,9,256]{3,1,2,0:T(8,128)S(1)} fusion(bf16[3,3,1024,256]{3,2,1,0:T(8,128)(2,1)S(1)} %bitcast.236, bf16[18,1,7,2,1024]{4,2,3,0,1:T(8,128)(2,1)S(1)} %slice.198, bf16[18,1,8,9,1024]{4,2,3,0,1:T(8,128)(2,1)S(1)} %copy.117, pred[8,9]{0,1:T(8,128)(4,1)S(1)} %copy-done.39), kind=kOutput, calls=%fused_computation.27 | convolution fusion | flops 5445844992 | bytes 9068616 | tf_op jit(solution)/shard_map/conv_general_dilated | solution.py:82
  97.1 1.4 %fusion.59 = bf16[16,64,256]{2,1,0:T(8,128)(2,1)} fusion(f32[16,1,64,256]{3,0,2,1:T(8,128)S(1)} %slice.199, f32[256]{0:T(256)S(1)} %bitcast.230), kind=kLoop, calls=%fused_computation.76 | loop fusion | flops 786432 | bytes 1573888 | tf_op jit(solution)/shard_map/convert_element_type | solution.py:296
  (276 shorter events, 35.0 us)
Async XLA Ops:
  0.0 47.0 %copy-start = (bf16[3,3,384,256]{3,2,1,0:T(8,128)(2,1)S(1)}, bf16[3,3,384,256]{3,2,1,0:T(8,128)(2,1)}, u32[]{:S(2)}) copy-start(bf16[3,3,384,256]{3,2,1,0:T(8,128)(2,1)} %param.22) | copy-start | bytes 5308420
  0.0 17.9 %copy-start.33 = (s32[50]{0:T(128)S(1)}, s32[50]{0:T(128)}, u32[]{:S(2)}) copy-start(s32[50]{0:T(128)} %constant.369) | copy-start | bytes 604
  0.0 17.9 %copy-start.34 = (s32[50]{0:T(128)S(1)}, s32[50]{0:T(128)}, u32[]{:S(2)}) copy-start(s32[50]{0:T(128)} %constant.357) | copy-start | bytes 604
  0.0 20.5 %copy-start.31 = (s32[50]{0:T(128)S(1)}, s32[50]{0:T(128)}, u32[]{:S(2)}) copy-start(s32[50]{0:T(128)} %constant.390) | copy-start | bytes 604
  0.0 20.5 %copy-start.32 = (s32[50]{0:T(128)S(1)}, s32[50]{0:T(128)}, u32[]{:S(2)}) copy-start(s32[50]{0:T(128)} %constant.378) | copy-start | bytes 604
  0.0 21.8 %copy-start.27 = (f32[50]{0:T(128)S(1)}, f32[50]{0:T(128)}, u32[]{:S(2)}) copy-start(f32[50]{0:T(128)} %constant.345) | copy-start | bytes 604
  0.0 21.8 %copy-start.28 = (f32[50]{0:T(128)S(1)}, f32[50]{0:T(128)}, u32[]{:S(2)}) copy-start(f32[50]{0:T(128)} %constant.344) | copy-start | bytes 604
  0.1 21.8 %copy-start.30 = (f32[50]{0:T(128)S(1)}, f32[50]{0:T(128)}, u32[]{:S(2)}) copy-start(f32[50]{0:T(128)} %constant.404) | copy-start | bytes 604
  0.1 21.8 %copy-start.37 = (f32[50]{0:T(128)S(1)}, f32[50]{0:T(128)}, u32[]{:S(2)}) copy-start(f32[50]{0:T(128)} %constant.403) | copy-start | bytes 604
  0.1 26.7 %copy-start.2 = (bf16[4,64,192]{2,1,0:T(8,128)(2,1)S(1)}, bf16[4,64,192]{2,1,0:T(8,128)(2,1)}, u32[]{:S(2)}) copy-start(bf16[4,64,192]{2,1,0:T(8,128)(2,1)} %param.19) | copy-start | bytes 294916
  0.1 27.4 %copy-start.1 = (f32[12,256]{1,0:T(8,128)S(1)}, f32[12,256]{1,0:T(8,128)}, u32[]{:S(2)}) copy-start(f32[12,256]{1,0:T(8,128)} %param.29) | copy-start | bytes 36868
  0.1 26.7 %copy-start.3 = (bf16[768,256]{1,0:T(8,128)(2,1)S(1)}, bf16[768,256]{1,0:T(8,128)(2,1)}, u32[]{:S(2)}) copy-start(bf16[768,256]{1,0:T(8,128)(2,1)} %param.26) | copy-start | bytes 1179652
  0.1 32.4 %collective-permute-start.7 = (bf16[2,32,384]{2,1,0:T(8,128)(2,1)}, bf16[2,32,384]{2,1,0:T(8,128)(2,1)S(1)}, u32[]{:S(2)}, u32[]{:S(2)}) collective-permute-start(bf16[2,32,384]{2,1,0:T(8,128)(2,1)} %param.20), channel_id=1, source_target_pairs={{0,4},{4,8},{8,12},{12,0},{1,5},{5,9},{9,13},{13,1},{2,6},{6,10},{... | collective-permute-start | bytes 147464 | tf_op jit(solution)/shard_map/ppermute | solution.py:125
  2.3 29.2 %collective-permute-start.1 = (bf16[4,20,192]{2,1,0:T(8,128)(2,1)}, bf16[4,20,192]{2,1,0:T(8,128)(2,1)}, u32[]{:S(2)}, u32[]{:S(2)}) collective-permute-start(bf16[4,20,192]{2,1,0:T(8,128)(2,1)} %get-tuple-element.13), channel_id=1, source_target_pairs={{0,2},{1,3},{2,0},{3,1},{4,6},{5,7},{6,4},{7,5},{8,10},{9,11},{10,... | collective-permute-start | bytes 92168 | tf_op jit(solution)/shard_map/ppermute | solution.py:30
  6.1 23.5 %collective-permute-start = (bf16[4,20,192]{2,1,0:T(8,128)(2,1)}, bf16[4,20,192]{2,1,0:T(8,128)(2,1)}, u32[]{:S(2)}, u32[]{:S(2)}) collective-permute-start(bf16[4,20,192]{2,1,0:T(8,128)(2,1)} %get-tuple-element.14), channel_id=1, source_target_pairs={{0,1},{1,2},{2,3},{3,0},{4,5},{5,6},{6,7},{7,4},{8,9},{9,10},{10,1... | collective-permute-start | bytes 92168 | tf_op jit(solution)/shard_map/ppermute | solution.py:30
  7.7 22.9 %collective-permute-start.2 = (bf16[4,20,192]{2,1,0:T(8,128)(2,1)}, bf16[4,20,192]{2,1,0:T(8,128)(2,1)}, u32[]{:S(2)}, u32[]{:S(2)}) collective-permute-start(bf16[4,20,192]{2,1,0:T(8,128)(2,1)} %get-tuple-element.15), channel_id=1, source_target_pairs={{0,3},{1,0},{2,1},{3,2},{4,7},{5,4},{6,5},{7,6},{8,11},{9,8},{10,9... | collective-permute-start | bytes 92168 | tf_op jit(solution)/shard_map/ppermute | solution.py:30
  17.8 22.3 %copy-start.5 = (bf16[2,32,384]{2,1,0:T(8,128)(2,1)S(1)}, bf16[2,32,384]{2,1,0:T(8,128)(2,1)}, u32[]{:S(2)}) copy-start(bf16[2,32,384]{2,1,0:T(8,128)(2,1)} %param.20) | copy-start | bytes 147460
  32.6 3.6 %collective-permute-start.8 = (bf16[2,32,384]{2,1,0:T(8,128)(2,1)S(1)}, bf16[2,32,384]{2,1,0:T(8,128)(2,1)S(1)}, u32[]{:S(2)}, u32[]{:S(2)}) collective-permute-start(bf16[2,32,384]{2,1,0:T(8,128)(2,1)S(1)} %collective-permute-done.7), channel_id=1, source_target_pairs={{0,4},{4,8},{8,12},{12,0},{1,5},{5,9},{9,13},{13,1},{2,6},{6,10},{... | collective-permute-start | bytes 147464 | tf_op jit(solution)/shard_map/ppermute | solution.py:125
  33.2 15.1 %collective-permute-start.4 = (bf16[232,256]{1,0:T(8,128)(2,1)S(1)}, bf16[232,256]{1,0:T(8,128)(2,1)S(1)}, u32[]{:S(2)}, u32[]{:S(2)}) collective-permute-start(bf16[232,256]{1,0:T(8,128)(2,1)S(1)} %pad_maximum_fusion.1), channel_id=1, source_target_pairs={{4,0},{8,4},{12,8},{5,1},{9,5},{13,9},{6,2},{10,6},{14,10},{7,3},{... | collective-permute-start | bytes 356360 | tf_op jit(solution)/shard_map/ppermute | solution.py:39
  36.1 3.9 %collective-permute-start.9 = (bf16[2,32,384]{2,1,0:T(8,128)(2,1)S(1)}, bf16[2,32,384]{2,1,0:T(8,128)(2,1)S(1)}, u32[]{:S(2)}, u32[]{:S(2)}) collective-permute-start(bf16[2,32,384]{2,1,0:T(8,128)(2,1)S(1)} %collective-permute-done.8), channel_id=1, source_target_pairs={{0,4},{4,8},{8,12},{12,0},{1,5},{5,9},{9,13},{13,1},{2,6},{6,10},{... | collective-permute-start | bytes 147464 | tf_op jit(solution)/shard_map/ppermute | solution.py:125
  36.4 11.9 %collective-permute-start.3 = (bf16[232,256]{1,0:T(8,128)(2,1)S(1)}, bf16[232,256]{1,0:T(8,128)(2,1)S(1)}, u32[]{:S(2)}, u32[]{:S(2)}) collective-permute-start(bf16[232,256]{1,0:T(8,128)(2,1)S(1)} %pad_maximum_fusion), channel_id=1, source_target_pairs={{0,4},{4,8},{8,12},{1,5},{5,9},{9,13},{2,6},{6,10},{10,14},{3,7},{... | collective-permute-start | bytes 356360 | tf_op jit(solution)/shard_map/ppermute | solution.py:39
  42.8 14.0 %collective-permute-start.11 = (bf16[50,256]{1,0:T(8,128)(2,1)S(1)}, bf16[50,256]{1,0:T(8,128)(2,1)S(1)}, u32[]{:S(2)}, u32[]{:S(2)}) collective-permute-start(bf16[50,256]{1,0:T(8,128)(2,1)S(1)} %pad_maximum_fusion.4), channel_id=1, source_target_pairs={{0,2},{1,3},{2,0},{3,1},{4,6},{5,7},{6,4},{7,5},{8,10},{9,11},{10,... | collective-permute-start | bytes 76808 | tf_op jit(solution)/shard_map/ppermute | solution.py:16
  42.9 13.9 %collective-permute-start.10 = (bf16[50,256]{1,0:T(8,128)(2,1)S(1)}, bf16[50,256]{1,0:T(8,128)(2,1)S(1)}, u32[]{:S(2)}, u32[]{:S(2)}) collective-permute-start(bf16[50,256]{1,0:T(8,128)(2,1)S(1)} %pad_maximum_fusion.4), channel_id=1, source_target_pairs={{0,1},{1,2},{2,3},{3,0},{4,5},{5,6},{6,7},{7,4},{8,9},{9,10},{10,1... | collective-permute-start | bytes 76808 | tf_op jit(solution)/shard_map/ppermute | solution.py:16
  43.4 13.3 %collective-permute-start.12 = (bf16[50,256]{1,0:T(8,128)(2,1)S(1)}, bf16[50,256]{1,0:T(8,128)(2,1)S(1)}, u32[]{:S(2)}, u32[]{:S(2)}) collective-permute-start(bf16[50,256]{1,0:T(8,128)(2,1)S(1)} %pad_maximum_fusion.4), channel_id=1, source_target_pairs={{0,3},{1,0},{2,1},{3,2},{4,7},{5,4},{6,5},{7,6},{8,11},{9,8},{10,9... | collective-permute-start | bytes 76808 | tf_op jit(solution)/shard_map/ppermute | solution.py:16
  49.7 18.4 %collective-permute-start.6 = (bf16[64,256]{1,0:T(8,128)(2,1)}, bf16[64,256]{1,0:T(8,128)(2,1)}, u32[]{:S(2)}, u32[]{:S(2)}) collective-permute-start(bf16[64,256]{1,0:T(8,128)(2,1)} %pad_maximum_fusion.3), channel_id=1, source_target_pairs={{1,0},{2,1},{3,2},{5,4},{6,5},{7,6},{9,8},{10,9},{11,10},{13,12},{... | collective-permute-start | bytes 98312 | tf_op jit(solution)/shard_map/ppermute | solution.py:39
  51.6 18.0 %collective-permute-start.5 = (bf16[64,256]{1,0:T(8,128)(2,1)}, bf16[64,256]{1,0:T(8,128)(2,1)}, u32[]{:S(2)}, u32[]{:S(2)}) collective-permute-start(bf16[64,256]{1,0:T(8,128)(2,1)} %pad_maximum_fusion.2), channel_id=1, source_target_pairs={{0,1},{1,2},{2,3},{4,5},{5,6},{6,7},{8,9},{9,10},{10,11},{12,13},{... | collective-permute-start | bytes 98312 | tf_op jit(solution)/shard_map/ppermute | solution.py:39
  57.6 9.4 %copy-start.9 = (f32[18,10]{1,0:T(8,128)S(1)}, f32[18,10]{1,0:T(8,128)}, u32[]{:S(2)}) copy-start(f32[18,10]{1,0:T(8,128)} %maximum_multiply_fusion.3) | copy-start | bytes 2164
  57.7 10.2 %copy-start.8 = (f32[66,34]{0,1:T(8,128)S(1)}, f32[66,34]{0,1:T(8,128)}, u32[]{:S(2)}) copy-start(f32[66,34]{0,1:T(8,128)} %maximum_multiply_fusion) | copy-start | bytes 26932
  59.1 12.0 %copy-start.23 = (f32[1,256]{1,0:T(1,128)S(1)}, f32[1,256]{1,0:T(1,128)}, u32[]{:S(2)}) copy-start(f32[1,256]{1,0:T(1,128)} %get-tuple-element.24) | copy-start | bytes 3076
  59.9 11.2 %collective-permute-start.13 = (bf16[6,12,256]{2,0,1:T(8,128)(2,1)}, bf16[6,12,256]{2,0,1:T(8,128)(2,1)S(1)}, u32[]{:S(2)}, u32[]{:S(2)}) collective-permute-start(bf16[6,12,256]{2,0,1:T(8,128)(2,1)} %get-tuple-element.16), channel_id=1, source_target_pairs={{0,1},{1,2},{2,3},{3,0},{4,5},{5,6},{6,7},{7,4},{8,9},{9,10},{10,1... | collective-permute-start | bytes 110600 | tf_op jit(solution)/shard_map/ppermute | solution.py:30
  59.9 11.2 %collective-permute-start.14 = (bf16[6,12,256]{2,0,1:T(8,128)(2,1)}, bf16[6,12,256]{2,0,1:T(8,128)(2,1)S(1)}, u32[]{:S(2)}, u32[]{:S(2)}) collective-permute-start(bf16[6,12,256]{2,0,1:T(8,128)(2,1)} %get-tuple-element.17), channel_id=1, source_target_pairs={{0,2},{1,3},{2,0},{3,1},{4,6},{5,7},{6,4},{7,5},{8,10},{9,11},{10,... | collective-permute-start | bytes 110600 | tf_op jit(solution)/shard_map/ppermute | solution.py:30
  61.0 10.1 %collective-permute-start.15 = (bf16[6,12,256]{2,0,1:T(8,128)(2,1)}, bf16[6,12,256]{2,0,1:T(8,128)(2,1)}, u32[]{:S(2)}, u32[]{:S(2)}) collective-permute-start(bf16[6,12,256]{2,0,1:T(8,128)(2,1)} %get-tuple-element.18), channel_id=1, source_target_pairs={{0,3},{1,0},{2,1},{3,2},{4,7},{5,4},{6,5},{7,6},{8,11},{9,8},{10,9... | collective-permute-start | bytes 110600 | tf_op jit(solution)/shard_map/ppermute | solution.py:30
  (31 other events, 136.9 us)
